TPU v7x, 32 devices: a whole 2x2x4 slice. The times are simulated.
32 devices in a mesh: dp: 8 (over z, x), tensor: 4 (over y, core).
Axes of the slice: x: 2, y: 2, z: 4, core: 2. Of those that a mesh axis runs over, the one named last changes fastest.
Arguments:
- tokens: bfloat16 [8192, 2048], P('dp'), may hold values from -6 to 6
- lengths: int32 [8], P('dp'), may hold values from 1 to 1024, 4915 in all
- norm_attn: float32 [2048], P('dp'), may hold values from 0.5 to 1.5
- query_proj: float32 [2048, 1024], P('dp', 'tensor'), may hold values from -0.125 to 0.125
- key_proj: float32 [2048, 1024], P('dp', 'tensor'), may hold values from -0.125 to 0.125
- value_proj: float32 [2048, 2048], P('dp', 'tensor'), may hold values from -0.125 to 0.125
- outgate_proj: float32 [2048, 2048], P('dp', 'tensor'), may hold values from -0.125 to 0.125
- rank_proj: float32 [2048, 16], P('dp'), may hold values from -0.125 to 0.125
- decay_proj: float32 [16, 4, 256], P(None, 'tensor', 'dp'), may hold values from -1.5 to 1.5
- decay_bias: float32 [4, 256], P('tensor', 'dp'), may hold values from -4 to 5
- head_gain: float32 [512], P('dp'), may hold values from 0.5 to 1.5
- out_proj: float32 [2048, 2048], P('tensor', 'dp'), may hold values from -0.25 to 0.25
- norm_ffn: float32 [2048], P('dp'), may hold values from 0.5 to 1.5
- gate_proj: float32 [2048, 5632], P('dp', 'tensor'), may hold values from -0.125 to 0.125
- up_proj: float32 [2048, 5632], P('dp', 'tensor'), may hold values from -0.125 to 0.125
- down_proj: float32 [5632, 2048], P('tensor', 'dp'), may hold values from -0.15625 to 0.15625
- cotangent: bfloat16 [8192, 2048], P('dp'), may hold values from -6 to 6
Outputs:
- output: bfloat16 [8192, 2048], P('dp')
- grad_tokens: bfloat16 [8192, 2048], P('dp')
- grad_norm_attn: float32 [2048], P('dp')
- grad_query_proj: float32 [2048, 1024], P('dp', 'tensor')
- grad_key_proj: float32 [2048, 1024], P('dp', 'tensor')
- grad_value_proj: float32 [2048, 2048], P('dp', 'tensor')
- grad_outgate_proj: float32 [2048, 2048], P('dp', 'tensor')
- grad_rank_proj: float32 [2048, 16], P('dp')
- grad_decay_proj: float32 [16, 4, 256], P(None, 'tensor', 'dp')
- grad_decay_bias: float32 [4, 256], P('tensor', 'dp')
- grad_head_gain: float32 [512], P('dp')
- grad_out_proj: float32 [2048, 2048], P('tensor', 'dp')
- grad_norm_ffn: float32 [2048], P('dp')
- grad_gate_proj: float32 [2048, 5632], P('dp', 'tensor')
- grad_up_proj: float32 [2048, 5632], P('dp', 'tensor')
- grad_down_proj: float32 [5632, 2048], P('tensor', 'dp')
Inputs may be any that keep to these rules, and one draw needn't show every extreme that they name: `lengths`: each slot's live positions come first; some slot is full.
All inputs are finite; a program needn't handle non-finite values. No bound on the sum of `lengths` on one device may be relied on, other than what follows from the above.
Results may differ from a plain program's by a relative error of at most 0.04.
Values may be sent and summed in bfloat16 or wider, within the bound.
A program may use at most 256 MiB of HBM per device.

v0:
```python
import jax
import jax.numpy as jnp
from jax import lax
from jax.sharding import PartitionSpec as P

DK = 256
DV = 512
GROUP = 64
SEQ_LEN = 1024
norm_eps = 1e-06
head_eps = 1.0
highest_precision = lax.Precision.HIGHEST


def rms_scale(values, gain):
    return values * lax.rsqrt(jnp.mean(values * values, axis=-1, keepdims=True) + norm_eps) * gain


def project(left, right):
    return jnp.dot(left, right, preferred_element_type=jnp.float32)


def collect(left, right):
    return lax.dot_general(
        left, right, (((0,), (0,)), ((), ())), preferred_element_type=jnp.float32
    )


def against(left, right):
    return lax.dot_general(
        left, right, (((1,), (1,)), ((), ())), preferred_element_type=jnp.float32
    )


def group_step(running_state, block):
    query_matrix, key_matrix, value_matrix, decay = block
    cumulative_decay = jnp.cumsum(decay, axis=1)
    steps = decay.shape[1]
    lower = (jnp.arange(steps)[:, None] >= jnp.arange(steps)[None, :]).astype(jnp.float32)
    spread = (
        jnp.exp(jnp.minimum(cumulative_decay[:, :, None, :] - cumulative_decay[:, None, :, :], 0.0))
        * lower[None, :, :, None]
    )
    weighted = query_matrix[:, :, None, :] * spread
    scores = jnp.einsum("hijk,hjk->hij", weighted, key_matrix, precision=highest_precision)
    inner = jnp.einsum("hij,hjv->hiv", scores, value_matrix, precision=highest_precision)
    outer_product = jnp.einsum(
        "muq,mqj->muj",
        query_matrix * jnp.exp(cumulative_decay),
        running_state,
        precision=highest_precision,
    )
    final_decay_row = cumulative_decay[:, -1:, :]
    carried_state = jnp.exp(final_decay_row[:, 0, :])[:, :, None] * running_state
    carried_state = carried_state + jnp.einsum(
        "zbm,zbi->zmi",
        key_matrix * jnp.exp(final_decay_row - cumulative_decay),
        value_matrix,
        precision=highest_precision,
    )
    return (carried_state, inner + outer_product)


def recurrence(query_matrix, key_matrix, value_matrix, decay):
    length = query_matrix.shape[0]
    heads = query_matrix.shape[1]
    count = length // GROUP

    def split(values):
        return jnp.transpose(values.reshape(count, GROUP, heads, values.shape[2]), (0, 2, 1, 3))

    start = jnp.zeros((heads, key_matrix.shape[2], value_matrix.shape[2]), jnp.float32)
    _, blocks = lax.scan(
        jax.checkpoint(group_step),
        start,
        (split(query_matrix), split(key_matrix), split(value_matrix), split(decay)),
    )
    return jnp.transpose(blocks, (0, 2, 1, 3)).reshape(length, heads, value_matrix.shape[2])


def mixer(
    query_matrix,
    key_matrix,
    value_matrix,
    outgate_rows,
    rank_rows,
    decay_weight,
    bias_weight,
    gain_weight,
):
    heads = bias_weight.shape[0]
    length = query_matrix.shape[0]
    seqs = length // SEQ_LEN
    before = jnp.dot(
        rank_rows,
        decay_weight.reshape(decay_weight.shape[0], -1),
        precision=highest_precision,
        preferred_element_type=jnp.float32,
    ) + bias_weight.reshape(-1)
    decay = jax.nn.log_sigmoid(before) / 16.0

    def arrange(values, width):
        return values.reshape(seqs, SEQ_LEN, heads, width)

    scale = DK ** (-0.5)
    mixed = jax.vmap(recurrence)(
        arrange(query_matrix * scale, DK),
        arrange(key_matrix, DK),
        arrange(value_matrix, DV),
        arrange(decay, DK),
    )
    mixed = mixed.reshape(length, heads, DV)
    normed = (
        mixed * lax.rsqrt(jnp.mean(mixed * mixed, axis=-1, keepdims=True) + head_eps) * gain_weight
    )
    return (normed * jax.nn.silu(outgate_rows.reshape(length, heads, DV))).reshape(
        length, heads * DV
    )


def swiglu(gate_rows, up_rows):
    return jax.nn.silu(gate_rows) * up_rows


def local(
    tokens,
    lengths,
    norm_attn,
    query_proj,
    key_proj,
    value_proj,
    outgate_proj,
    rank_proj,
    decay_proj,
    decay_bias,
    head_gain,
    out_proj,
    norm_ffn,
    gate_proj,
    up_proj,
    down_proj,
    cotangent,
):
    half = jnp.bfloat16
    (
        gain_attn,
        query_full,
        key_full,
        value_full,
        outgate_full,
        rank_full,
        decay_full,
        bias_full,
        head_full,
        out_full,
    ) = (
        lax.all_gather(norm_attn.astype(half), "dp", axis=0, tiled=True),
        lax.all_gather(query_proj.astype(half), "dp", axis=0, tiled=True),
        lax.all_gather(key_proj.astype(half), "dp", axis=0, tiled=True),
        lax.all_gather(value_proj.astype(half), "dp", axis=0, tiled=True),
        lax.all_gather(outgate_proj.astype(half), "dp", axis=0, tiled=True),
        lax.all_gather(rank_proj.astype(half), "dp", axis=0, tiled=True),
        lax.all_gather(decay_proj.astype(half), "dp", axis=2, tiled=True),
        lax.all_gather(decay_bias.astype(half), "dp", axis=1, tiled=True),
        lax.all_gather(head_gain.astype(half), "dp", axis=0, tiled=True),
        lax.all_gather(out_proj.astype(half), "dp", axis=1, tiled=True),
    )
    rows_total = tokens.shape[0]
    positions = jnp.arange(SEQ_LEN, dtype=jnp.int32)
    mask = (positions[None, :] < lengths[:, None]).astype(jnp.float32).reshape(rows_total, 1)
    tokens_full = tokens.astype(jnp.float32)
    normed, pull_first = jax.vjp(rms_scale, tokens_full, gain_attn.astype(jnp.float32))
    normed_half = normed.astype(half)
    query_matrix = project(normed_half, query_full)
    key_matrix = project(normed_half, key_full)
    value_matrix = project(normed_half, value_full)
    outgate_rows = project(normed_half, outgate_full)
    rank_rows = project(normed_half, rank_full)
    gated, pull_mix = jax.vjp(
        mixer,
        query_matrix,
        key_matrix,
        value_matrix,
        outgate_rows,
        rank_rows,
        decay_full.astype(jnp.float32),
        bias_full.astype(jnp.float32),
        head_full.astype(jnp.float32),
    )
    gated_half = gated.astype(half)
    attn = lax.psum(project(gated_half, out_full), "tensor")
    middle = tokens_full + attn
    gain_ffn, gate_full, up_full, down_full = (
        lax.all_gather(norm_ffn.astype(half), "dp", axis=0, tiled=True),
        lax.all_gather(gate_proj.astype(half), "dp", axis=0, tiled=True),
        lax.all_gather(up_proj.astype(half), "dp", axis=0, tiled=True),
        lax.all_gather(down_proj.astype(half), "dp", axis=1, tiled=True),
    )
    normed_ffn, pull_second = jax.vjp(rms_scale, middle, gain_ffn.astype(jnp.float32))
    normed_ffn_half = normed_ffn.astype(half)
    gate_rows = project(normed_ffn_half, gate_full)
    up_rows = project(normed_ffn_half, up_full)
    hidden, pull_glu = jax.vjp(swiglu, gate_rows, up_rows)
    hidden_half = hidden.astype(half)
    ffn = lax.psum(project(hidden_half, down_full).astype(jnp.bfloat16), "tensor").astype(
        jnp.float32
    )
    output = (mask * (middle + ffn)).astype(half)
    d_out = cotangent.astype(jnp.float32) * mask
    d_out_half = d_out.astype(half)
    gain_ffn, gate_full, up_full, down_full = (
        lax.all_gather(norm_ffn.astype(half), "dp", axis=0, tiled=True),
        lax.all_gather(gate_proj.astype(half), "dp", axis=0, tiled=True),
        lax.all_gather(up_proj.astype(half), "dp", axis=0, tiled=True),
        lax.all_gather(down_proj.astype(half), "dp", axis=1, tiled=True),
    )
    grad_down = collect(hidden_half, d_out_half)
    d_hidden = against(d_out_half, down_full)
    d_gate, d_up = pull_glu(d_hidden)
    d_gate_half = d_gate.astype(half)
    d_up_half = d_up.astype(half)
    grad_gate = collect(normed_ffn_half, d_gate_half)
    grad_up = collect(normed_ffn_half, d_up_half)
    d_normed_ffn = lax.psum(
        (against(d_gate_half, gate_full) + against(d_up_half, up_full)).astype(jnp.bfloat16),
        "tensor",
    ).astype(jnp.float32)
    d_middle_norm, grad_gain_ffn = pull_second(d_normed_ffn)
    grad_norm_ffn, grad_gate_proj, grad_up_proj, grad_down_proj = (
        lax.psum_scatter(
            grad_gain_ffn.astype(jnp.bfloat16), "dp", scatter_dimension=0, tiled=True
        ).astype(jnp.float32),
        lax.psum_scatter(
            grad_gate.astype(jnp.bfloat16), "dp", scatter_dimension=0, tiled=True
        ).astype(jnp.float32),
        lax.psum_scatter(
            grad_up.astype(jnp.bfloat16), "dp", scatter_dimension=0, tiled=True
        ).astype(jnp.float32),
        lax.psum_scatter(
            grad_down.astype(jnp.bfloat16), "dp", scatter_dimension=1, tiled=True
        ).astype(jnp.float32),
    )
    d_middle = d_out + d_middle_norm
    d_attn_half = d_middle.astype(half)
    (
        gain_attn,
        query_full,
        key_full,
        value_full,
        outgate_full,
        rank_full,
        decay_full,
        bias_full,
        head_full,
        out_full,
    ) = (
        lax.all_gather(norm_attn.astype(half), "dp", axis=0, tiled=True),
        lax.all_gather(query_proj.astype(half), "dp", axis=0, tiled=True),
        lax.all_gather(key_proj.astype(half), "dp", axis=0, tiled=True),
        lax.all_gather(value_proj.astype(half), "dp", axis=0, tiled=True),
        lax.all_gather(outgate_proj.astype(half), "dp", axis=0, tiled=True),
        lax.all_gather(rank_proj.astype(half), "dp", axis=0, tiled=True),
        lax.all_gather(decay_proj.astype(half), "dp", axis=2, tiled=True),
        lax.all_gather(decay_bias.astype(half), "dp", axis=1, tiled=True),
        lax.all_gather(head_gain.astype(half), "dp", axis=0, tiled=True),
        lax.all_gather(out_proj.astype(half), "dp", axis=1, tiled=True),
    )
    grad_out = collect(gated_half, d_attn_half)
    d_gated = against(d_attn_half, out_full)
    d_query, d_key, d_value, d_outgate, d_rank, grad_decay, grad_bias, grad_head = pull_mix(d_gated)
    d_query_half = d_query.astype(half)
    d_key_half = d_key.astype(half)
    d_value_half = d_value.astype(half)
    d_outgate_half = d_outgate.astype(half)
    grad_query = collect(normed_half, d_query_half)
    grad_key = collect(normed_half, d_key_half)
    grad_value = collect(normed_half, d_value_half)
    grad_outgate = collect(normed_half, d_outgate_half)
    d_normed_part = (
        against(d_query_half, query_full)
        + against(d_key_half, key_full)
        + against(d_value_half, value_full)
        + against(d_outgate_half, outgate_full)
    )
    d_normed, d_rank_total, grad_head_total = (
        lax.psum(d_normed_part.astype(jnp.bfloat16), "tensor").astype(jnp.float32),
        lax.psum(d_rank.astype(jnp.bfloat16), "tensor").astype(jnp.float32),
        lax.psum(grad_head.astype(jnp.bfloat16), "tensor").astype(jnp.float32),
    )
    d_rank_half = d_rank_total.astype(half)
    grad_rank = collect(normed_half, d_rank_half)
    d_normed = d_normed + against(d_rank_half, rank_full)
    d_tokens_norm, grad_gain_attn = pull_first(d_normed)
    grad_tokens = (d_middle + d_tokens_norm).astype(half)
    (
        grad_norm_attn,
        grad_query_proj,
        grad_key_proj,
        grad_value_proj,
        grad_outgate_proj,
        grad_rank_proj,
        grad_decay_proj,
        grad_decay_bias,
        grad_head_gain,
        grad_out_proj,
    ) = (
        lax.psum_scatter(
            grad_gain_attn.astype(jnp.bfloat16), "dp", scatter_dimension=0, tiled=True
        ).astype(jnp.float32),
        lax.psum_scatter(
            grad_query.astype(jnp.bfloat16), "dp", scatter_dimension=0, tiled=True
        ).astype(jnp.float32),
        lax.psum_scatter(
            grad_key.astype(jnp.bfloat16), "dp", scatter_dimension=0, tiled=True
        ).astype(jnp.float32),
        lax.psum_scatter(
            grad_value.astype(jnp.bfloat16), "dp", scatter_dimension=0, tiled=True
        ).astype(jnp.float32),
        lax.psum_scatter(
            grad_outgate.astype(jnp.bfloat16), "dp", scatter_dimension=0, tiled=True
        ).astype(jnp.float32),
        lax.psum_scatter(
            grad_rank.astype(jnp.bfloat16), "dp", scatter_dimension=0, tiled=True
        ).astype(jnp.float32),
        lax.psum_scatter(
            grad_decay.astype(jnp.bfloat16), "dp", scatter_dimension=2, tiled=True
        ).astype(jnp.float32),
        lax.psum_scatter(
            grad_bias.astype(jnp.bfloat16), "dp", scatter_dimension=1, tiled=True
        ).astype(jnp.float32),
        lax.psum_scatter(
            grad_head_total.astype(jnp.bfloat16), "dp", scatter_dimension=0, tiled=True
        ).astype(jnp.float32),
        lax.psum_scatter(
            grad_out.astype(jnp.bfloat16), "dp", scatter_dimension=1, tiled=True
        ).astype(jnp.float32),
    )
    return (
        output,
        grad_tokens,
        grad_norm_attn,
        grad_query_proj,
        grad_key_proj,
        grad_value_proj,
        grad_outgate_proj,
        grad_rank_proj,
        grad_decay_proj,
        grad_decay_bias,
        grad_head_gain,
        grad_out_proj,
        grad_norm_ffn,
        grad_gate_proj,
        grad_up_proj,
        grad_down_proj,
    )


def solution(mesh):
    return jax.shard_map(
        local,
        mesh=mesh,
        in_specs=(
            P("dp", None),
            P("dp"),
            P("dp"),
            P("dp", "tensor"),
            P("dp", "tensor"),
            P("dp", "tensor"),
            P("dp", "tensor"),
            P("dp", None),
            P(None, "tensor", "dp"),
            P("tensor", "dp"),
            P("dp"),
            P("tensor", "dp"),
            P("dp"),
            P("dp", "tensor"),
            P("dp", "tensor"),
            P("tensor", "dp"),
            P("dp", None),
        ),
        out_specs=(
            P("dp", None),
            P("dp", None),
            P("dp"),
            P("dp", "tensor"),
            P("dp", "tensor"),
            P("dp", "tensor"),
            P("dp", "tensor"),
            P("dp", None),
            P(None, "tensor", "dp"),
            P("tensor", "dp"),
            P("dp"),
            P("tensor", "dp"),
            P("dp"),
            P("dp", "tensor"),
            P("dp", "tensor"),
            P("tensor", "dp"),
        ),
        check_vma=False,
    )
```

profile of v0, /device:TPU:0, one launch (start us, length us, event | category | flops | bytes accessed | tf_op | source)
XLA Modules:
  0.0 2493.8 jit_solution(15633964255061561891)
XLA Ops:
  19.4 22.3 all-gather
  41.7 30.6 %all_gather.52 = bf16[2048,16]{0,1:T(8,128)(2,1)S(1)} all-gather(bf16[256,16]{0,1:T(8,128)(2,1)S(1)} %convert_element_type.283), channel_id=1, replica_groups=mesh['dp'=8,'tensor'=4] {'dp'}, dimensions={0}, use_global_device_ids=true | all-gather | bytes 73728 | tf_op jit(solution)/shard_map/all_gather | solution.py:162
  74.7 17.5 all-reduce.7
  92.4 30.9 %all_gather.53 = bf16[16,1,256]{0,1,2:T(2,128)(2,1)S(1)} all-gather(bf16[16,1,32]{0,1,2:T(2,128)(2,1)S(1)} %copy.93), channel_id=1, replica_groups=mesh['dp'=8,'tensor'=4] {'dp'}, dimensions={2}, use_global_device_ids=true | all-gather | bytes 9216 | tf_op jit(solution)/shard_map/all_gather | solution.py:163
  153.0 229.3 %while.40 = (s32[]{:T(128)}, f32[1,1,256,512]{3,2,1,0:T(8,128)S(1)}, f32[16,1,1,64,512]{4,3,2,1,0:T(8,128)S(1)}, f32[16,1,1,256,512]{4,3,2,1,0:T(8,128)}, f32[16...) while((s32[]{:T(128)}, ...), condition=%wide.region_3.4_spmd.clone.clone, body=%wide.region_1.3_spmd.clone.sunk.clone | while | flops 245047296 | bytes 12723313 | solution.py:73
  402.8 18.1 all-gather.1
  421.6 127.8 %all-reduce.13.cloned.1.call-done = f32[1024,2048]{1,0:T(8,128)} async-done(((f32[1024,2048]{1,0:T(8,128)}), f32[1024,2048]{1,0:T(8,128)}) %all-reduce.13.cloned.1.call-update) | async-done | bytes 8388624 | tf_op jit(solution)/shard_map/psum | solution.py:191
  561.1 82.9 %all-gather.21.cloned.1.call-done = bf16[2048,1408]{1,0:T(8,128)(2,1)} async-done(((bf16[256,1408]{1,0:T(8,128)(2,1)}), bf16[2048,1408]{1,0:T(8,128)(2,1)}) %all-gather.21.cloned.1.call-update) | async-done | bytes 5767184 | tf_op jit(solution)/shard_map/all_gather | solution.py:195
  656.2 80.5 %all-gather.23.cloned.1.call-done = bf16[2048,1408]{1,0:T(8,128)(2,1)} async-done(((bf16[256,1408]{1,0:T(8,128)(2,1)}), bf16[2048,1408]{1,0:T(8,128)(2,1)}) %all-gather.23.cloned.1.call-update) | async-done | bytes 5767184 | tf_op jit(solution)/shard_map/all_gather | solution.py:196
  748.4 81.7 %all-gather.25.cloned.1.call-done = bf16[1408,2048]{1,0:T(8,128)(2,1)} async-done(((bf16[1408,256]{1,0:T(8,128)(2,1)}), bf16[1408,2048]{1,0:T(8,128)(2,1)}) %all-gather.25.cloned.1.call-update) | async-done | bytes 5767184 | tf_op jit(solution)/shard_map/all_gather | solution.py:197
  867.1 81.9 %all-reduce.15.cloned.1.call-done = bf16[1024,2048]{1,0:T(8,128)(2,1)} async-done(((bf16[1024,2048]{1,0:T(8,128)(2,1)}), bf16[1024,2048]{1,0:T(8,128)(2,1)}) %all-reduce.15.cloned.1.call-update) | async-done | bytes 4194320 | tf_op jit(solution)/shard_map/psum | solution.py:224
  969.6 466.3 %while.41 = (s32[]{:T(128)}, f32[1,1,256,512]{2,3,1,0:T(8,128)S(1)}, f32[16,1,1,64,256]{4,3,2,1,0:T(8,128)S(1)}, bf16[16,1,1,64,256]{4,3,2,1,0:T(8,128)(2,1)}, b...) while((s32[]{:T(128)}, ...), condition=%wide.region_19.20_spmd.clone.clone, body=%wide.region_11.19_spmd.clone.sunk.clone | while | flops 502210560 | bytes 24297648 | solution.py:73
  1559.2 23.8 reduce-scatter.34.cloned.1.call-done
  1584.4 56.2 %reduce-scatter.24.cloned.1.call-done = bf16[256,16]{0,1:T(8,128)(2,1)} async-done(((bf16[2048,16]{0,1:T(8,128)(2,1)}), bf16[256,16]{0,1:T(8,128)(2,1)}) %reduce-scatter.24.cloned.1.call-update) | async-done | bytes 8208 | tf_op jit(solution)/shard_map/reduce_scatter | solution.py:322
  1641.8 65.8 %reduce-scatter.16.cloned.1.call-done = bf16[256,256]{1,0:T(8,128)(2,1)} async-done(((bf16[2048,256]{1,0:T(8,128)(2,1)}), bf16[256,256]{1,0:T(8,128)(2,1)}) %reduce-scatter.16.cloned.1.call-update) | async-done | bytes 131088 | tf_op jit(solution)/shard_map/reduce_scatter | solution.py:310
  1709.2 65.5 %reduce-scatter.18.cloned.1.call-done = bf16[256,256]{1,0:T(8,128)(2,1)} async-done(((bf16[2048,256]{1,0:T(8,128)(2,1)}), bf16[256,256]{1,0:T(8,128)(2,1)}) %reduce-scatter.18.cloned.1.call-update) | async-done | bytes 131088 | tf_op jit(solution)/shard_map/reduce_scatter | solution.py:313
  1776.3 152.7 %all-reduce.17.cloned.1.call-done = (bf16[1024,2048]{1,0:T(8,128)(2,1)}, bf16[1024,2048]{1,0:T(8,128)(2,1)}) async-done(((bf16[1024,2048]{1,0:T(8,128)(2,1)}, bf16[1024,2048]{1,0:T(8,128)(2,1)}), (bf16[1024,2048]{1,0:T(8,128)(2,1)}, bf16[1024,2048]{1,0:T(8,128)(2,1)})) %all-reduce.17.cloned.1.call-update) | async-done | bytes 8388624 | tf_op jit(solution)/shard_map/psum | solution.py:205
  1936.4 22.3 all-reduce.6
  1965.2 36.4 %reduce-scatter.26.cloned.1.call-done = bf16[512,256]{1,0:T(8,128)(2,1)} async-done(((bf16[512,2048]{1,0:T(8,128)(2,1)}), bf16[512,256]{1,0:T(8,128)(2,1)}) %reduce-scatter.26.cloned.1.call-update) | async-done | bytes 262160 | tf_op jit(solution)/shard_map/reduce_scatter | solution.py:334
  2003.4 69.1 %reduce-scatter.20.cloned.1.call-done = bf16[256,512]{1,0:T(8,128)(2,1)} async-done(((bf16[2048,512]{1,0:T(8,128)(2,1)}), bf16[256,512]{1,0:T(8,128)(2,1)}) %reduce-scatter.20.cloned.1.call-update) | async-done | bytes 262160 | tf_op jit(solution)/shard_map/reduce_scatter | solution.py:316
  2074.2 69.1 %reduce-scatter.22.cloned.1.call-done = bf16[256,512]{1,0:T(8,128)(2,1)} async-done(((bf16[2048,512]{1,0:T(8,128)(2,1)}), bf16[256,512]{1,0:T(8,128)(2,1)}) %reduce-scatter.22.cloned.1.call-update) | async-done | bytes 262160 | tf_op jit(solution)/shard_map/reduce_scatter | solution.py:319
  2161.6 94.9 %reduce-scatter.28.cloned.1.call-done = bf16[256,1408]{1,0:T(8,128)(2,1)} async-done(((bf16[2048,1408]{1,0:T(8,128)(2,1)}), bf16[256,1408]{1,0:T(8,128)(2,1)}) %reduce-scatter.28.cloned.1.call-update) | async-done | bytes 720912 | tf_op jit(solution)/shard_map/reduce_scatter | solution.py:233
  2258.8 111.3 %reduce-scatter.30.cloned.1.call-done = bf16[256,1408]{1,0:T(8,128)(2,1)} async-done(((bf16[2048,1408]{1,0:T(8,128)(2,1)}), bf16[256,1408]{1,0:T(8,128)(2,1)}) %reduce-scatter.30.cloned.1.call-update) | async-done | bytes 720912 | tf_op jit(solution)/shard_map/reduce_scatter | solution.py:236
  2372.5 111.8 %reduce-scatter.32.cloned.1.call-done = bf16[1408,256]{1,0:T(8,128)(2,1)} async-done(((bf16[1408,2048]{1,0:T(8,128)(2,1)}), bf16[1408,256]{1,0:T(8,128)(2,1)}) %reduce-scatter.32.cloned.1.call-update) | async-done | bytes 720912 | tf_op jit(solution)/shard_map/reduce_scatter | solution.py:239
  (926 shorter events, 1019.1 us)
Async XLA Ops:
  7.2 125.4 %all-gather.15.cloned.1.call-start = ((), (), s32[]{:S(2)}) async-start(), calls=%async_computation.13 | async-start | bytes 1179648 | tf_op jit(solution)/shard_map/all_gather | solution.py:158
  8.9 128.4 %all-gather.11.cloned.1.call-start = ((), (), s32[]{:S(2)}) async-start(), calls=%async_computation.11 | async-start | bytes 1179648 | tf_op jit(solution)/shard_map/all_gather | solution.py:159
  10.6 135.9 %all-gather.13.cloned.1.call-start = ((), (), s32[]{:S(2)}) async-start(), calls=%async_computation.12 | async-start | bytes 2359296 | tf_op jit(solution)/shard_map/all_gather | solution.py:160
  12.5 370.2 %all-gather.17.cloned.1.call-start = ((), (), s32[]{:S(2)}) async-start(), calls=%async_computation.14 | async-start | bytes 2359296 | tf_op jit(solution)/shard_map/all_gather | solution.py:161
  14.3 375.9 %all-gather.19.cloned.1.call-start = ((), (), s32[]{:S(2)}) async-start(), calls=%async_computation.15 | async-start | bytes 2359296 | tf_op jit(solution)/shard_map/all_gather | solution.py:166
  16.2 533.2 %all-reduce.13.cloned.1.call-start = ((), (), s32[]{:S(2)}) async-start(), calls=%async_computation.16 | async-start | bytes 16777216 | tf_op jit(solution)/shard_map/psum | solution.py:191
  397.8 246.2 %all-gather.21.cloned.1.call-start = ((), (), s32[]{:S(2)}) async-start(), calls=%async_computation.17 | async-start | bytes 6488064 | tf_op jit(solution)/shard_map/all_gather | solution.py:195
  400.1 336.6 %all-gather.23.cloned.1.call-start = ((), (), s32[]{:S(2)}) async-start(), calls=%async_computation.18 | async-start | bytes 6488064 | tf_op jit(solution)/shard_map/all_gather | solution.py:196
  401.2 428.9 %all-gather.25.cloned.1.call-start = ((), (), s32[]{:S(2)}) async-start(), calls=%async_computation.19 | async-start | bytes 6488064 | tf_op jit(solution)/shard_map/all_gather | solution.py:197
  402.7 546.3 %all-reduce.15.cloned.1.call-start = ((), (), s32[]{:S(2)}) async-start(), calls=%async_computation.20 | async-start | bytes 8388608 | tf_op jit(solution)/shard_map/psum | solution.py:224
  865.2 692.7 %reduce-scatter.36.cloned.1.call-start = ((), (), s32[]{:S(2)}) async-start(), calls=%async_computation.31 | async-start | bytes 73728
  1454.6 128.4 %reduce-scatter.34.cloned.1.call-start = ((), (), s32[]{:S(2)}) async-start(), calls=%async_computation.30 | async-start | bytes 73728
  1456.0 184.5 %reduce-scatter.24.cloned.1.call-start = ((), (), s32[]{:S(2)}) async-start(), calls=%async_computation.25 | async-start | bytes 73728 | tf_op jit(solution)/shard_map/reduce_scatter | solution.py:322
  1456.8 250.8 %reduce-scatter.16.cloned.1.call-start = ((), (), s32[]{:S(2)}) async-start(), calls=%async_computation.21 | async-start | bytes 1179648 | tf_op jit(solution)/shard_map/reduce_scatter | solution.py:310
  1461.3 313.4 %reduce-scatter.18.cloned.1.call-start = ((), (), s32[]{:S(2)}) async-start(), calls=%async_computation.22 | async-start | bytes 1179648 | tf_op jit(solution)/shard_map/reduce_scatter | solution.py:313
  1474.8 454.2 %all-reduce.17.cloned.1.call-start = ((), (), s32[]{:S(2)}) async-start(), calls=%async_computation.32 | async-start | bytes 16777216 | tf_op jit(solution)/shard_map/psum | solution.py:205
  1499.2 502.4 %reduce-scatter.26.cloned.1.call-start = ((), (), s32[]{:S(2)}) async-start(), calls=%async_computation.26 | async-start | bytes 2359296 | tf_op jit(solution)/shard_map/reduce_scatter | solution.py:334
  1507.5 564.9 %reduce-scatter.20.cloned.1.call-start = ((), (), s32[]{:S(2)}) async-start(), calls=%async_computation.23 | async-start | bytes 2359296 | tf_op jit(solution)/shard_map/reduce_scatter | solution.py:316
  1513.5 629.9 %reduce-scatter.22.cloned.1.call-start = ((), (), s32[]{:S(2)}) async-start(), calls=%async_computation.24 | async-start | bytes 2359296 | tf_op jit(solution)/shard_map/reduce_scatter | solution.py:319
  1519.7 736.8 %reduce-scatter.28.cloned.1.call-start = ((), (), s32[]{:S(2)}) async-start(), calls=%async_computation.27 | async-start | bytes 6488064 | tf_op jit(solution)/shard_map/reduce_scatter | solution.py:233
  1530.9 839.3 %reduce-scatter.30.cloned.1.call-start = ((), (), s32[]{:S(2)}) async-start(), calls=%async_computation.28 | async-start | bytes 6488064 | tf_op jit(solution)/shard_map/reduce_scatter | solution.py:236
  1543.6 940.7 %reduce-scatter.32.cloned.1.call-start = ((), (), s32[]{:S(2)}) async-start(), calls=%async_computation.29 | async-start | bytes 6488064 | tf_op jit(solution)/shard_map/reduce_scatter | solution.py:239
  1556.5 372.6 %copy-start.25 = (f32[8,1,256]{2,1,0:T(1,128)S(1)}, f32[8,1,256]{2,1,0:T(1,128)}, u32[]{:S(2)}) copy-start(f32[8,1,256]{2,1,0:T(1,128)} %copy-done.24) | copy-start | bytes 24580
  1556.5 372.6 %copy-start.29 = (f32[1024]{0:T(1024)S(1)}, f32[1024]{0:T(1024)}, u32[]{:S(2)}) copy-start(f32[1024]{0:T(1024)} %copy-done.28) | copy-start | bytes 12292
  (45 other events, 1430.8 us)
Sparse Core Ops, SparseCore 0:
  10.7 43.2 all-gather.14
  56.7 38.8 all-gather.10
  98.3 48.2 all-gather.12
  149.1 47.6 all-gather.16
  199.3 49.1 all-gather.18
  397.9 151.4 all-reduce.12
  551.5 92.4 all-gather.20
  646.2 90.4 all-gather.22
  738.7 91.3 all-gather.24
  865.3 83.6 all-reduce.14
  1454.7 62.8 reduce-scatter.35
  1521.5 61.4 reduce-scatter.33
  1586.7 53.8 reduce-scatter.23
  1644.4 63.1 reduce-scatter.15
  1711.4 63.2 reduce-scatter.17
  1777.2 151.8 all-reduce.16
  1932.4 69.1 reduce-scatter.25
  2005.0 67.3 reduce-scatter.19
  2076.0 67.3 reduce-scatter.21
  2146.9 109.6 reduce-scatter.27
  2260.2 109.9 reduce-scatter.29
  2373.8 110.3 reduce-scatter.31
where the time goes:
time: 2510 us; the launch traced here: 2490 us
  waiting for transfers between devices  1320 us (53%)
  matrix products  647 us (26%)
  other arithmetic  210 us (8%)
  blocking collectives  158 us (6%)
  local copies, waits for them, and re-layouts  139 us (6%)
    dot_general x48, matrix products, group_step(): jnp.einsum('hijk,hjk->hij', weighted, key_matrix, precision=highest_preci...  316 us
    psum x1, waiting for transfers between devices, local(): lax.psum(project(hidden_half, down_full).astype(jnp.bfloat16), 'tensor')  153 us
    psum x1, waiting for transfers between devices, local(): attn = lax.psum(project(gated_half, out_full), 'tensor')  128 us
    reduce_scatter x1, waiting for transfers between devices, local(): lax.psum_scatter(grad_down.astype(jnp.bfloat16), 'dp', scatter_dimension=...  112 us
    reduce_scatter x1, waiting for transfers between devices, local(): lax.psum_scatter(grad_up.astype(jnp.bfloat16), 'dp', scatter_dimension=0,...  111 us
    reduce_scatter x1, waiting for transfers between devices, local(): lax.psum_scatter(grad_gate.astype(jnp.bfloat16), 'dp', scatter_dimension=...  94.9 us
    all_gather x1, waiting for transfers between devices, local(): lax.all_gather(gate_proj.astype(half), 'dp', axis=0, tiled=True)  82.9 us
    psum x1, waiting for transfers between devices, local(): lax.psum((against(d_gate_half, gate_full) + against(d_up_half, up_full))....  81.9 us
  transfers between devices with their start and end apart: 22, of which 17 were waited for; matrix products, arithmetic and copies ran while one was open for 18% of the time, Pallas kernels for 0%

commit v1 on v0

--- a/solution.py
+++ b/solution.py
@@ -1,3 +1,4 @@
+import functools
 import jax
 import jax.numpy as jnp
 from jax import lax
@@ -10,6 +11,14 @@
 norm_eps = 1e-06
 head_eps = 1.0
 highest_precision = lax.Precision.HIGHEST
+
+
+def _supply_all_sectors(matrix, across):
+    state_next = lax.all_gather(matrix, across).sum(axis=0)
+    return state_next
+
+
+pair_gates = functools.partial(_supply_all_sectors, across="tensor")
 
 
 def rms_scale(values, gain):
@@ -221,9 +230,8 @@
     d_up_half = d_up.astype(half)
     grad_gate = collect(normed_ffn_half, d_gate_half)
     grad_up = collect(normed_ffn_half, d_up_half)
-    d_normed_ffn = lax.psum(
-        (against(d_gate_half, gate_full) + against(d_up_half, up_full)).astype(jnp.bfloat16),
-        "tensor",
+    d_normed_ffn = pair_gates(
+        (against(d_gate_half, gate_full) + against(d_up_half, up_full)).astype(jnp.bfloat16)
     ).astype(jnp.float32)
     d_middle_norm, grad_gain_ffn = pull_second(d_normed_ffn)
     grad_norm_ffn, grad_gate_proj, grad_up_proj, grad_down_proj = (

time: 2510 us -> 2200 us (0.88)
  waiting for transfers between devices: 1320 us -> 998 us
    reduce_scatter x1, waiting for transfers between devices: 112 us -> 0.01 us  [local(): lax.psum_scatter(grad_down.astype(jnp.bfloat16), 'dp', scatter_dimension=...]
    reduce_scatter x1, waiting for transfers between devices: 111 us -> 0.01 us  [local(): lax.psum_scatter(grad_up.astype(jnp.bfloat16), 'dp', scatter_dimension=0,...]
    reduce_scatter x1, waiting for transfers between devices: 94.9 us -> 0.02 us  [local(): lax.psum_scatter(grad_gate.astype(jnp.bfloat16), 'dp', scatter_dimension=...]
    psum x1 -> x0, waiting for transfers between devices: 81.9 us -> none  [local(): lax.psum((against(d_gate_half, gate_full) + against(d_up_half, up_full))....]
    all_gather x0 -> x1, waiting for transfers between devices: none -> 68.1 us  [_supply_all_sectors(): state_next = lax.all_gather(matrix, across).sum(axis=0)]
    unnamed x24, waiting for transfers between devices: 24.7 us -> 54.9 us
  transfers between devices with their start and end apart: 22 -> 22, of which waited for: 17 -> 14; matrix products, arithmetic and copies ran while one was open for 18% -> 43% of each run, Pallas kernels for 0% -> 0%
where the time goes in v1:
time: 2200 us; the launch traced here: 2190 us
  waiting for transfers between devices  998 us (45%)
  matrix products  648 us (29%)
  other arithmetic  222 us (10%)
  blocking collectives  159 us (7%)
  local copies, waits for them, and re-layouts  137 us (6%)
    dot_general x48, matrix products, group_step(): jnp.einsum('hijk,hjk->hij', weighted, key_matrix, precision=highest_preci...  317 us
    psum x1, waiting for transfers between devices, local(): lax.psum(project(hidden_half, down_full).astype(jnp.bfloat16), 'tensor')  153 us
    psum x1, waiting for transfers between devices, local(): attn = lax.psum(project(gated_half, out_full), 'tensor')  128 us
    all_gather x1, waiting for transfers between devices, local(): lax.all_gather(gate_proj.astype(half), 'dp', axis=0, tiled=True)  82.9 us
    all_gather x1, waiting for transfers between devices, local(): lax.all_gather(down_proj.astype(half), 'dp', axis=1, tiled=True)  81.7 us
    all_gather x1, waiting for transfers between devices, local(): lax.all_gather(up_proj.astype(half), 'dp', axis=0, tiled=True)  80.7 us
    reduce_scatter x1, waiting for transfers between devices, local(): lax.psum_scatter(grad_value.astype(jnp.bfloat16), 'dp', scatter_dimension...  69.1 us
    dot_general x9, matrix products, against(): lax.dot_general(left, right, (((1,), (1,)), ((), ())), preferred_element_...  68.9 us
  transfers between devices with their start and end apart: 22, of which 14 were waited for; matrix products, arithmetic and copies ran while one was open for 43% of the time, Pallas kernels for 0%

profile of v1, /device:TPU:0, one launch (start us, length us, event | category | flops | bytes accessed | tf_op | source)
XLA Modules:
  0.0 2186.6 jit_solution(9842876419639555176)
XLA Ops:
  19.4 22.3 %all-gather.1 = bf16[8,1,256]{2,1,0:T(2,128)(2,1)S(1)} all-gather(bf16[1,1,256]{2,1,0:T(2,128)(2,1)S(1)} %reshape.739), channel_id=1, replica_groups=mesh['dp'=8,'tensor'=4] {'dp'}, dimensions={0}, use_global_device_ids=true | all-gather | bytes 4608 | tf_op jit(solution)/shard_map/all_gather | solution.py:166
  41.7 30.6 %all_gather.58 = bf16[2048,16]{0,1:T(8,128)(2,1)S(1)} all-gather(bf16[256,16]{0,1:T(8,128)(2,1)S(1)} %convert_element_type.285), channel_id=1, replica_groups=mesh['dp'=8,'tensor'=4] {'dp'}, dimensions={0}, use_global_device_ids=true | all-gather | bytes 73728 | tf_op jit(solution)/shard_map/all_gather | solution.py:171
  74.7 17.5 all-reduce.7
  92.4 30.9 %all_gather.59 = bf16[16,1,256]{0,1,2:T(2,128)(2,1)S(1)} all-gather(bf16[16,1,32]{0,1,2:T(2,128)(2,1)S(1)} %copy.93), channel_id=1, replica_groups=mesh['dp'=8,'tensor'=4] {'dp'}, dimensions={2}, use_global_device_ids=true | all-gather | bytes 9216 | tf_op jit(solution)/shard_map/all_gather | solution.py:172
  153.1 229.4 %while.40 = (s32[]{:T(128)}, f32[1,1,256,512]{3,2,1,0:T(8,128)S(1)}, f32[16,1,1,64,512]{4,3,2,1,0:T(8,128)S(1)}, f32[16,1,1,256,512]{4,3,2,1,0:T(8,128)}, f32[16...) while((s32[]{:T(128)}, ...), condition=%wide.region_3.4_spmd.clone.clone, body=%wide.region_1.3_spmd.clone.sunk.clone | while | flops 245047296 | bytes 12723313 | solution.py:82
  402.8 18.1 all-gather.2
  421.6 127.8 %all-reduce.12.cloned.1.call-done = f32[1024,2048]{1,0:T(8,128)} async-done(((f32[1024,2048]{1,0:T(8,128)}), f32[1024,2048]{1,0:T(8,128)}) %all-reduce.12.cloned.1.call-update) | async-done | bytes 8388624 | tf_op jit(solution)/shard_map/psum | solution.py:200
  561.2 82.9 %all-gather.23.cloned.1.call-done = bf16[2048,1408]{1,0:T(8,128)(2,1)} async-done(((bf16[256,1408]{1,0:T(8,128)(2,1)}), bf16[2048,1408]{1,0:T(8,128)(2,1)}) %all-gather.23.cloned.1.call-update) | async-done | bytes 5767184 | tf_op jit(solution)/shard_map/all_gather | solution.py:204
  656.1 80.7 %all-gather.25.cloned.1.call-done = bf16[2048,1408]{1,0:T(8,128)(2,1)} async-done(((bf16[256,1408]{1,0:T(8,128)(2,1)}), bf16[2048,1408]{1,0:T(8,128)(2,1)}) %all-gather.25.cloned.1.call-update) | async-done | bytes 5767184 | tf_op jit(solution)/shard_map/all_gather | solution.py:205
  748.5 81.7 %all-gather.27.cloned.1.call-done = bf16[1408,2048]{1,0:T(8,128)(2,1)} async-done(((bf16[1408,256]{1,0:T(8,128)(2,1)}), bf16[1408,2048]{1,0:T(8,128)(2,1)}) %all-gather.27.cloned.1.call-update) | async-done | bytes 5767184 | tf_op jit(solution)/shard_map/all_gather | solution.py:206
  830.2 15.8 multiply_convert_fusion.2
  876.6 12.1 convolution_convert_fusion.1
  901.5 68.1 %all-gather.29.cloned.1.call-done = bf16[4096,2048]{1,0:T(8,128)(2,1)} async-done(((bf16[1024,2048]{1,0:T(8,128)(2,1)}), bf16[4096,2048]{1,0:T(8,128)(2,1)}) %all-gather.29.cloned.1.call-update) | async-done | bytes 16777232 | tf_op jit(solution)/shard_map/all_gather | solution.py:17
  969.5 12.1 reduce_sum.158
  1002.5 467.7 %while.41 = (s32[]{:T(128)}, f32[1,1,256,512]{2,3,1,0:T(8,128)S(1)}, f32[16,1,1,64,256]{4,3,2,1,0:T(8,128)S(1)}, bf16[16,1,1,64,256]{4,3,2,1,0:T(8,128)(2,1)}, b...) while((s32[]{:T(128)}, ...), condition=%wide.region_19.20_spmd.clone.clone, body=%wide.region_11.19_spmd.clone.sunk.clone | while | flops 502210560 | bytes 24297648 | solution.py:82
  1564.0 54.2 %reduce-scatter.34.cloned.1.call-done = bf16[32,16]{1,0:T(8,128)(2,1)} async-done(((bf16[256,16]{1,0:T(8,128)(2,1)}), bf16[32,16]{1,0:T(8,128)(2,1)}) %reduce-scatter.34.cloned.1.call-update) | async-done | bytes 1040
  1619.6 56.0 %reduce-scatter.24.cloned.1.call-done = bf16[256,16]{0,1:T(8,128)(2,1)} async-done(((bf16[2048,16]{0,1:T(8,128)(2,1)}), bf16[256,16]{0,1:T(8,128)(2,1)}) %reduce-scatter.24.cloned.1.call-update) | async-done | bytes 8208 | tf_op jit(solution)/shard_map/reduce_scatter | solution.py:330
  1676.9 65.2 %reduce-scatter.16.cloned.1.call-done = bf16[256,256]{1,0:T(8,128)(2,1)} async-done(((bf16[2048,256]{1,0:T(8,128)(2,1)}), bf16[256,256]{1,0:T(8,128)(2,1)}) %reduce-scatter.16.cloned.1.call-update) | async-done | bytes 131088 | tf_op jit(solution)/shard_map/reduce_scatter | solution.py:318
  1743.7 64.8 %reduce-scatter.18.cloned.1.call-done = bf16[256,256]{1,0:T(8,128)(2,1)} async-done(((bf16[2048,256]{1,0:T(8,128)(2,1)}), bf16[256,256]{1,0:T(8,128)(2,1)}) %reduce-scatter.18.cloned.1.call-update) | async-done | bytes 131088 | tf_op jit(solution)/shard_map/reduce_scatter | solution.py:321
  1810.1 153.4 %all-reduce.14.cloned.1.call-done = (bf16[1024,2048]{1,0:T(8,128)(2,1)}, bf16[1024,2048]{1,0:T(8,128)(2,1)}) async-done(((bf16[1024,2048]{1,0:T(8,128)(2,1)}, bf16[1024,2048]{1,0:T(8,128)(2,1)}), (bf16[1024,2048]{1,0:T(8,128)(2,1)}, bf16[1024,2048]{1,0:T(8,128)(2,1)})) %all-reduce.14.cloned.1.call-update) | async-done | bytes 8388624 | tf_op jit(solution)/shard_map/psum | solution.py:214
  1970.7 22.5 %all-reduce.6 = (bf16[2048]{0:T(1024)(128)(2,1)S(1)}, bf16[512]{0:T(512)(128)(2,1)S(1)}, bf16[2048]{0:T(1024)(128)(2,1)S(1)}) all-reduce(bf16[2048]{0:T(1024)(128)(2,1)S(1)} %get-tuple-element.576, bf16[512]{0:T(512)(128)(2,1)S(1)} %get-tuple-element.578, ...), channel_id=3, replica_groups=mesh['dp'=8,'tensor'=4] {'dp'}, use_global_device_ids=true, to_apply=%region_24.25.clone | all-reduce | flops 4608 | bytes 18432
  1999.8 36.1 %reduce-scatter.26.cloned.1.call-done = bf16[512,256]{1,0:T(8,128)(2,1)} async-done(((bf16[512,2048]{1,0:T(8,128)(2,1)}), bf16[512,256]{1,0:T(8,128)(2,1)}) %reduce-scatter.26.cloned.1.call-update) | async-done | bytes 262160 | tf_op jit(solution)/shard_map/reduce_scatter | solution.py:342
  2037.7 69.1 %reduce-scatter.20.cloned.1.call-done = bf16[256,512]{1,0:T(8,128)(2,1)} async-done(((bf16[2048,512]{1,0:T(8,128)(2,1)}), bf16[256,512]{1,0:T(8,128)(2,1)}) %reduce-scatter.20.cloned.1.call-update) | async-done | bytes 262160 | tf_op jit(solution)/shard_map/reduce_scatter | solution.py:324
  2125.0 52.7 %reduce-scatter.22.cloned.1.call-done = bf16[256,512]{1,0:T(8,128)(2,1)} async-done(((bf16[2048,512]{1,0:T(8,128)(2,1)}), bf16[256,512]{1,0:T(8,128)(2,1)}) %reduce-scatter.22.cloned.1.call-update) | async-done | bytes 262160 | tf_op jit(solution)/shard_map/reduce_scatter | solution.py:327
  (933 shorter events, 990.3 us)
Async XLA Ops:
  7.2 125.4 %all-gather.17.cloned.1.call-start = ((), (), s32[]{:S(2)}) async-start(), calls=%async_computation.13 | async-start | bytes 1179648 | tf_op jit(solution)/shard_map/all_gather | solution.py:167
  8.9 128.5 %all-gather.13.cloned.1.call-start = ((), (), s32[]{:S(2)}) async-start(), calls=%async_computation.11 | async-start | bytes 1179648 | tf_op jit(solution)/shard_map/all_gather | solution.py:168
  10.6 135.9 %all-gather.15.cloned.1.call-start = ((), (), s32[]{:S(2)}) async-start(), calls=%async_computation.12 | async-start | bytes 2359296 | tf_op jit(solution)/shard_map/all_gather | solution.py:169
  12.5 370.4 %all-gather.19.cloned.1.call-start = ((), (), s32[]{:S(2)}) async-start(), calls=%async_computation.14 | async-start | bytes 2359296 | tf_op jit(solution)/shard_map/all_gather | solution.py:170
  14.3 376.0 %all-gather.21.cloned.1.call-start = ((), (), s32[]{:S(2)}) async-start(), calls=%async_computation.15 | async-start | bytes 2359296 | tf_op jit(solution)/shard_map/all_gather | solution.py:175
  16.2 533.3 %all-reduce.12.cloned.1.call-start = ((), (), s32[]{:S(2)}) async-start(), calls=%async_computation.16 | async-start | bytes 16777216 | tf_op jit(solution)/shard_map/psum | solution.py:200
  397.9 246.2 %all-gather.23.cloned.1.call-start = ((), (), s32[]{:S(2)}) async-start(), calls=%async_computation.17 | async-start | bytes 6488064 | tf_op jit(solution)/shard_map/all_gather | solution.py:204
  400.2 336.6 %all-gather.25.cloned.1.call-start = ((), (), s32[]{:S(2)}) async-start(), calls=%async_computation.18 | async-start | bytes 6488064 | tf_op jit(solution)/shard_map/all_gather | solution.py:205
  401.2 429.0 %all-gather.27.cloned.1.call-start = ((), (), s32[]{:S(2)}) async-start(), calls=%async_computation.19 | async-start | bytes 6488064 | tf_op jit(solution)/shard_map/all_gather | solution.py:206
  402.7 566.8 %all-gather.29.cloned.1.call-start = ((), (), s32[]{:S(2)}) async-start(), calls=%async_computation.29 | async-start | bytes 20971520 | tf_op jit(solution)/shard_map/all_gather | solution.py:17
  865.3 690.5 %reduce-scatter.28.cloned.1.call-start = ((), (), s32[]{:S(2)}) async-start(), calls=%async_computation.26 | async-start | bytes 6488064 | tf_op jit(solution)/shard_map/reduce_scatter | solution.py:241
  876.5 681.6 %reduce-scatter.30.cloned.1.call-start = ((), (), s32[]{:S(2)}) async-start(), calls=%async_computation.27 | async-start | bytes 6488064 | tf_op jit(solution)/shard_map/reduce_scatter | solution.py:244
  888.7 671.7 %reduce-scatter.32.cloned.1.call-start = ((), (), s32[]{:S(2)}) async-start(), calls=%async_computation.28 | async-start | bytes 6488064 | tf_op jit(solution)/shard_map/reduce_scatter | solution.py:247
  901.4 661.3 %reduce-scatter.36.cloned.1.call-start = ((), (), s32[]{:S(2)}) async-start(), calls=%async_computation.31 | async-start | bytes 73728
  1489.3 128.9 %reduce-scatter.34.cloned.1.call-start = ((), (), s32[]{:S(2)}) async-start(), calls=%async_computation.30 | async-start | bytes 73728
  1490.7 184.9 %reduce-scatter.24.cloned.1.call-start = ((), (), s32[]{:S(2)}) async-start(), calls=%async_computation.24 | async-start | bytes 73728 | tf_op jit(solution)/shard_map/reduce_scatter | solution.py:330
  1491.3 250.8 %reduce-scatter.16.cloned.1.call-start = ((), (), s32[]{:S(2)}) async-start(), calls=%async_computation.20 | async-start | bytes 1179648 | tf_op jit(solution)/shard_map/reduce_scatter | solution.py:318
  1495.9 312.5 %reduce-scatter.18.cloned.1.call-start = ((), (), s32[]{:S(2)}) async-start(), calls=%async_computation.21 | async-start | bytes 1179648 | tf_op jit(solution)/shard_map/reduce_scatter | solution.py:321
  1509.4 454.1 %all-reduce.14.cloned.1.call-start = ((), (), s32[]{:S(2)}) async-start(), calls=%async_computation.32 | async-start | bytes 16777216 | tf_op jit(solution)/shard_map/psum | solution.py:214
  1533.8 502.1 %reduce-scatter.26.cloned.1.call-start = ((), (), s32[]{:S(2)}) async-start(), calls=%async_computation.25 | async-start | bytes 2359296 | tf_op jit(solution)/shard_map/reduce_scatter | solution.py:342
  1542.2 564.7 %reduce-scatter.20.cloned.1.call-start = ((), (), s32[]{:S(2)}) async-start(), calls=%async_computation.22 | async-start | bytes 2359296 | tf_op jit(solution)/shard_map/reduce_scatter | solution.py:324
  1548.1 629.6 %reduce-scatter.22.cloned.1.call-start = ((), (), s32[]{:S(2)}) async-start(), calls=%async_computation.23 | async-start | bytes 2359296 | tf_op jit(solution)/shard_map/reduce_scatter | solution.py:327
  1554.4 409.1 %copy-start.23 = (bf16[2048,16]{0,1:T(8,128)(2,1)S(1)}, bf16[2048,16]{0,1:T(8,128)(2,1)}, u32[]{:S(2)}) copy-start(bf16[2048,16]{0,1:T(8,128)(2,1)} %copy-done.22) | copy-start | bytes 196612
  1554.4 409.1 %copy-start.25 = (f32[8,1,256]{2,1,0:T(1,128)S(1)}, f32[8,1,256]{2,1,0:T(1,128)}, u32[]{:S(2)}) copy-start(f32[8,1,256]{2,1,0:T(1,128)} %copy-done.24) | copy-start | bytes 24580
  (48 other events, 1674.9 us)
Sparse Core Ops, SparseCore 0:
  10.7 43.2 all-gather.16
  56.7 38.8 all-gather.12
  98.3 48.2 all-gather.14
  149.1 47.6 all-gather.18
  199.2 49.1 all-gather.20
  398.0 151.4 all-reduce.11
  551.6 92.4 all-gather.22
  646.3 90.4 all-gather.24
  738.8 91.3 all-gather.26
  865.4 104.0 all-gather.28
  973.2 110.5 reduce-scatter.27
  1087.3 109.9 reduce-scatter.29
  1201.0 110.3 reduce-scatter.31
  1489.4 63.3 reduce-scatter.35
  1556.7 61.4 reduce-scatter.33
  1621.7 53.8 reduce-scatter.23
  1678.8 63.1 reduce-scatter.15
  1745.3 63.0 reduce-scatter.17
  1811.6 151.8 all-reduce.13
  1966.8 69.0 reduce-scatter.25
  2039.5 67.2 reduce-scatter.19
  2110.3 67.3 reduce-scatter.21
